TPU v7x, 32 devices: a whole 2x2x4 slice. The times are simulated.
32 devices in a mesh: layer: 4 (over y, core), shard: 8 (over z, x).
Axes of the slice: x: 2, y: 2, z: 4, core: 2. Of those that a mesh axis runs over, the one named last changes fastest.
Arguments:
- input_acts: bfloat16 [8, 4096, 5120], P('layer', 'shard'), may hold values from -6 to 6
- output_grads: bfloat16 [8, 4096, 1024], P('layer', 'shard'), may hold values from -6 to 6
- input_inverse: bfloat16 [8, 5120, 5120], P('layer', 'shard'), may hold values from -1 to 2, as said below
- output_inverse: bfloat16 [8, 1024, 1024], P('layer', 'shard'), may hold values from -1 to 2, as said below
- query_input: bfloat16 [8, 5120, 512], P(None, 'shard'), may hold values from -0.0048828125 to 0.0048828125
- query_output: bfloat16 [8, 1024, 512], P(None, 'shard'), may hold values from -0.1875 to 0.1875
- layer_order: int32 [8], replicated, may hold values from 0 to 7, each once
Outputs:
- scores: float32 [4096, 16], P('shard', 'layer')
Inputs may be any that keep to these rules, and one draw needn't show every extreme that they name: `input_inverse`: symmetric in its last two dimensions, with a unit-sized diagonal. `output_inverse`: symmetric in its last two dimensions, with a unit-sized diagonal.
All inputs are finite; a program needn't handle non-finite values.
Results may differ from a plain program's by a relative error of at most 0.0045.
Values may be sent and summed in bfloat16 or wider, within the bound.
No kernel may reach another device: no remote copies, remote signals or barrier semaphores. Data moves between devices by JAX's collectives and lax.ppermute only.
A program may use at most 128 MiB of HBM per device.

v0:
```python
import jax
import jax.numpy as jnp
from jax import lax
from jax.sharding import PartitionSpec as P

QUERIES = 16


def shards(
    input_acts, output_grads, input_inverse, output_inverse, query_input, query_output, layer_order
):
    depth = input_acts.shape[0]
    tokens = input_acts.shape[1]
    first = lax.axis_index("layer") * depth
    chosen_in = []
    chosen_out = []
    for position in range(depth):
        model_layer = layer_order[first + position]
        chosen_in.append(lax.dynamic_index_in_dim(query_input, model_layer, 0, keepdims=False))
        chosen_out.append(lax.dynamic_index_in_dim(query_output, model_layer, 0, keepdims=False))
    vectors_in = jnp.stack(chosen_in, axis=1)
    vectors_out = jnp.stack(chosen_out, axis=1)
    width = vectors_in.shape[2]
    whole_in = lax.all_gather(vectors_in, "shard", axis=0, tiled=True)
    folded_in = jnp.einsum(
        "jsk,kjn->sjn", input_inverse, whole_in, preferred_element_type=jnp.float32
    ).astype(jnp.bfloat16)
    columns = input_acts
    left = jnp.einsum(
        "jti,ijn->jtn",
        columns,
        lax.all_gather(folded_in, "shard", axis=0, tiled=True),
        preferred_element_type=jnp.float32,
    )
    whole_out = lax.all_gather(vectors_out, "shard", axis=0, tiled=True)
    folded_out = jnp.einsum(
        "jsk,kjn->sjn", output_inverse, whole_out, preferred_element_type=jnp.float32
    ).astype(jnp.bfloat16)
    columns = output_grads
    right = jnp.einsum(
        "jti,ijn->jtn",
        columns,
        lax.all_gather(folded_out, "shard", axis=0, tiled=True),
        preferred_element_type=jnp.float32,
    )
    product = (left * right).reshape(depth, tokens, QUERIES, width // QUERIES).sum(axis=(0, 3))
    return lax.psum_scatter(product, "layer", scatter_dimension=1, tiled=True)


def solution(mesh):
    in_specs = (
        P("layer", "shard", None),
        P("layer", "shard", None),
        P("layer", "shard", None),
        P("layer", "shard", None),
        P(None, "shard", None),
        P(None, "shard", None),
        P(),
    )
    out_specs = P("shard", "layer")
    return jax.shard_map(shards, mesh=mesh, in_specs=in_specs, out_specs=out_specs, check_vma=False)
```

profile of v0, /device:TPU:0, one launch (start us, length us, event | category | flops | bytes accessed | tf_op | source)
XLA Modules:
  0.0 442.9 jit_solution(11020521583007273015)
XLA Ops:
  6.5 0.0 copy-start
  6.5 0.0 all-gather.5.cloned.1.call-start
  6.5 1.5 fusion.2
  11.8 2.2 constant_dynamic-slice_fusion.3
  14.0 0.3 copy.8
  14.3 1.4 copy.9
  15.7 1.3 pad_maximum_fusion
  17.0 0.0 all-gather.5.cloned.1.call-update
  17.0 0.0 all-gather.9.cloned.1.call-start
  17.1 1.0 constant_dynamic-slice_fusion.1
  18.1 0.1 copy.10
  18.2 0.1 copy.11
  18.3 0.7 pad_maximum_fusion.1
  19.0 0.0 all-gather.9.cloned.1.call-update
  19.1 0.0 copy-start.1
  19.1 0.0 all-gather.7.cloned.1.call-start
  19.1 150.9 %all-gather.5.cloned.1.call-done = bf16[5120,2,512]{0,2,1:T(8,128)(2,1)} async-done(((bf16[640,2,512]{0,2,1:T(8,128)(2,1)}), bf16[5120,2,512]{0,2,1:T(8,128)(2,1)}) %all-gather.5.cloned.1.call-update) | async-done | bytes 10485776 | tf_op jit(solution)/shard_map/all_gather | solution.py:24
  170.0 15.7 %fusion = bf16[640,2,512]{0,2,1:T(8,128)(2,1)} fusion(bf16[5120,2,512]{0,2,1:T(8,128)(2,1)} %all-gather.5.cloned.1.call-done, bf16[2,640,5120]{2,1,0:T(8,128)(2,1)} %param.9), kind=kOutput, calls=%fused_computation.2 | convolution fusion | flops 6711541760 | bytes 24903680 | tf_op jit(solution)/shard_map/jsk,kjn->sjn/dot_general | solution.py:25
  185.7 0.0 copy-start.2
  185.7 0.0 all-gather.7.cloned.1.call-update
  185.7 0.0 all-gather.11.cloned.1.call-start
  185.8 34.8 %all-gather.9.cloned.1.call-done = bf16[1024,2,512]{0,2,1:T(8,128)(2,1)} async-done(((bf16[128,2,512]{0,2,1:T(8,128)(2,1)}), bf16[1024,2,512]{0,2,1:T(8,128)(2,1)}) %all-gather.9.cloned.1.call-update) | async-done | bytes 2097168 | tf_op jit(solution)/shard_map/all_gather | solution.py:35
  220.6 0.0 copy-done.1
  220.6 3.0 fusion.1
  223.6 0.0 all-gather.11.cloned.1.call-update
  223.7 0.0 copy-done.2
  223.7 0.6 dynamic-slice
  224.9 146.3 %all-gather.7.cloned.1.call-done = bf16[5120,2,512]{0,2,1:T(8,128)(2,1)} async-done(((bf16[640,2,512]{0,2,1:T(8,128)(2,1)}), bf16[5120,2,512]{0,2,1:T(8,128)(2,1)}) %all-gather.7.cloned.1.call-update) | async-done | bytes 10485776 | tf_op jit(solution)/shard_map/all_gather | solution.py:32
  371.2 12.4 %fusion.3 = f32[2,512,512]{2,1,0:T(8,128)} fusion(bf16[5120,2,512]{0,2,1:T(8,128)(2,1)} %all-gather.7.cloned.1.call-done, bf16[2,512,5120]{2,1,0:T(8,128)(2,1)} %param.7), kind=kOutput, calls=%fused_computation.14 | convolution fusion | flops 5368709120 | bytes 23068672 | tf_op jit(solution)/shard_map/jti,ijn->jtn/dot_general | solution.py:29
  383.5 38.1 %all-gather.11.cloned.1.call-done = bf16[1024,2,512]{0,2,1:T(8,128)(2,1)} async-done(((bf16[128,2,512]{0,2,1:T(8,128)(2,1)}), bf16[1024,2,512]{0,2,1:T(8,128)(2,1)}) %all-gather.11.cloned.1.call-update) | async-done | bytes 2097168 | tf_op jit(solution)/shard_map/all_gather | solution.py:43
  421.6 0.0 copy-done
  421.6 3.6 multiply_reduce_fusion
  425.2 0.2 bitcast_reduce_fusion
  425.4 10.4 %all-reduce = f32[512,16]{0,1:T(8,128)S(1)} all-reduce(f32[512,16]{0,1:T(8,128)S(1)} %bitcast_reduce_fusion), channel_id=2, replica_groups=mesh['layer'=4,'shard'=8] {'layer'}, use_global_device_ids=true, to_apply=%region_2.3.clone | all-reduce | flops 8192 | bytes 65536
  435.8 0.6 constant_dynamic-slice_fusion.4
Async XLA Ops:
  6.5 415.1 %copy-start = (bf16[2,512,1024]{2,1,0:T(8,128)(2,1)S(1)}, bf16[2,512,1024]{2,1,0:T(8,128)(2,1)}, u32[]{:S(2)}) copy-start(bf16[2,512,1024]{2,1,0:T(8,128)(2,1)} %param.8) | copy-start | bytes 6291460
  6.5 163.5 %all-gather.5.cloned.1.call-start = ((), (), s32[]{:S(2)}) async-start(), calls=%async_computation | async-start | bytes 11796480 | tf_op jit(solution)/shard_map/all_gather | solution.py:24
  17.0 203.6 %all-gather.9.cloned.1.call-start = ((), (), s32[]{:S(2)}) async-start(), calls=%async_computation.2 | async-start | bytes 2359296 | tf_op jit(solution)/shard_map/all_gather | solution.py:35
  19.1 201.5 %copy-start.1 = (bf16[2,128,1024]{2,1,0:T(8,128)(2,1)S(1)}, bf16[2,128,1024]{2,1,0:T(8,128)(2,1)}, u32[]{:S(2)}) copy-start(bf16[2,128,1024]{2,1,0:T(8,128)(2,1)} %param.10) | copy-start | bytes 1572868
  19.1 352.1 %all-gather.7.cloned.1.call-start = ((), (), s32[]{:S(2)}) async-start(), calls=%async_computation.1 | async-start | bytes 11796480 | tf_op jit(solution)/shard_map/all_gather | solution.py:32
  185.7 38.0 %copy-start.2 = (u32[32]{0:T(128)S(1)}, u32[32]{0:T(128)}, u32[]{:S(2)}) copy-start(u32[32]{0:T(128)} %constant.35) | copy-start | bytes 388
  185.7 235.9 %all-gather.11.cloned.1.call-start = ((), (), s32[]{:S(2)}) async-start(), calls=%async_computation.3 | async-start | bytes 2359296 | tf_op jit(solution)/shard_map/all_gather | solution.py:43
Sparse Core Ops, SparseCore 0:
  17.1 152.8 all-gather.4
  172.1 48.5 all-gather.8
  222.8 148.2 all-gather.6
  373.1 48.5 all-gather.10
where the time goes:
time: 443 us
  waiting for transfers between devices  370 us (84%)
  matrix products  34.7 us (8%)
  between operations  17.7 us (4%)
  blocking collectives  10.4 us (2%)
  local copies, waits for them, and re-layouts  7.78 us (2%)
    all_gather x1, waiting for transfers between devices, shards(): whole_in = lax.all_gather(vectors_in, 'shard', axis=0, tiled=True)  151 us
    all_gather x1, waiting for transfers between devices, shards(): lax.all_gather(folded_in, 'shard', axis=0, tiled=True)  146 us
    all_gather x1, waiting for transfers between devices, shards(): lax.all_gather(folded_out, 'shard', axis=0, tiled=True)  38.1 us
    all_gather x1, waiting for transfers between devices, shards(): whole_out = lax.all_gather(vectors_out, 'shard', axis=0, tiled=True)  34.8 us
    dot_general x1, matrix products, shards(): jnp.einsum('jsk,kjn->sjn', input_inverse, whole_in, preferred_element_typ...  15.7 us
    dot_general x1, matrix products, shards(): jnp.einsum('jti,ijn->jtn', columns, lax.all_gather(folded_in, 'shard', ax...  12.4 us
    unnamed x1, blocking collectives  10.4 us
  transfers between devices with their start and end apart: 4, of which 4 were waited for; matrix products, arithmetic and copies ran while one was open for 8% of the time, Pallas kernels for 0%

commit v1 on v0

--- a/solution.py
+++ b/solution.py
@@ -37,12 +37,41 @@
         "jsk,kjn->sjn", output_inverse, whole_out, preferred_element_type=jnp.float32
     ).astype(jnp.bfloat16)
     columns = output_grads
+    length, position_2, width_2 = (
+        lax.axis_size("shard"),
+        lax.axis_index("shard"),
+        folded_out.shape[0],
+    )
+    route = [(i, (i + 1) % length) for i in range(length)]
+    backward = [(i, (i - 1) % length) for i in range(length)]
+    half = length // 2
+    from_left = from_right = folded_out
     right = jnp.einsum(
         "jti,ijn->jtn",
-        columns,
-        lax.all_gather(folded_out, "shard", axis=0, tiled=True),
+        lax.dynamic_slice_in_dim(columns, position_2 * width_2, folded_out.shape[0], axis=2),
+        folded_out,
         preferred_element_type=jnp.float32,
     )
+    for step in range(1, half + 1):
+        from_left = lax.ppermute(from_left, "shard", route)
+        if step < length - half:
+            from_right = lax.ppermute(from_right, "shard", backward)
+            right = right + jnp.einsum(
+                "jti,ijn->jtn",
+                lax.dynamic_slice_in_dim(
+                    columns, (position_2 + step) % length * width_2, from_right.shape[0], axis=2
+                ),
+                from_right,
+                preferred_element_type=jnp.float32,
+            )
+        right = right + jnp.einsum(
+            "jti,ijn->jtn",
+            lax.dynamic_slice_in_dim(
+                columns, (position_2 - step) % length * width_2, from_left.shape[0], axis=2
+            ),
+            from_left,
+            preferred_element_type=jnp.float32,
+        )
     product = (left * right).reshape(depth, tokens, QUERIES, width // QUERIES).sum(axis=(0, 3))
     return lax.psum_scatter(product, "layer", scatter_dimension=1, tiled=True)
 

time: 443 us -> 423 us (0.955)
  waiting for transfers between devices: 370 us -> 323 us
  starting transfers between devices: 0.13 us -> 13.7 us
  matrix products: 34.7 us -> 48.2 us
    all_gather x1, waiting for transfers between devices: 146 us -> 108 us  [shards(): lax.all_gather(folded_in, 'shard', axis=0, tiled=True)]
    all_gather x1 -> x0, waiting for transfers between devices: 38.1 us -> none  [shards(): lax.all_gather(folded_out, 'shard', axis=0, tiled=True)]
    ppermute x0 -> x7, waiting for transfers between devices: none -> 30.9 us  [the longest x4 30.3 us: shards(): from_left = lax.ppermute(from_left, 'shard', route)]
    dot_general x1 -> x8, matrix products: 3.61 us -> 17.7 us  [the longest x7 15.9 us: shards(): jnp.einsum('jti,ijn->jtn', lax.dynamic_slice_in_dim(columns, (position_2...]
    ppermute x0 -> x7, starting transfers between devices: none -> 13.6 us  [the longest x3 7.1 us: shards(): from_right = lax.ppermute(from_right, 'shard', backward)]
  transfers between devices with their start and end apart: 4 -> 10, of which waited for: 4 -> 7; matrix products, arithmetic and copies ran while one was open for 8% -> 11% of each run, Pallas kernels for 0% -> 0%
where the time goes in v1:
time: 423 us
  waiting for transfers between devices  323 us (76%)
  matrix products  48.2 us (11%)
  between operations  17.6 us (4%)
  starting transfers between devices  13.7 us (3%)
  blocking collectives  10.3 us (2%)
  local copies, waits for them, and re-layouts  7.75 us (2%)
    all_gather x1, waiting for transfers between devices, shards(): whole_in = lax.all_gather(vectors_in, 'shard', axis=0, tiled=True)  151 us
    all_gather x1, waiting for transfers between devices, shards(): lax.all_gather(folded_in, 'shard', axis=0, tiled=True)  108 us
    all_gather x1, waiting for transfers between devices, shards(): whole_out = lax.all_gather(vectors_out, 'shard', axis=0, tiled=True)  33.5 us
    ppermute x4, waiting for transfers between devices, shards(): from_left = lax.ppermute(from_left, 'shard', route)  30.3 us
    dot_general x7, matrix products, shards(): jnp.einsum('jti,ijn->jtn', lax.dynamic_slice_in_dim(columns, (position_2...  15.9 us
    dot_general x1, matrix products, shards(): jnp.einsum('jsk,kjn->sjn', input_inverse, whole_in, preferred_element_typ...  15.7 us
    dot_general x1, matrix products, shards(): jnp.einsum('jti,ijn->jtn', columns, lax.all_gather(folded_in, 'shard', ax...  12.5 us
    unnamed x1, blocking collectives  10.3 us
  transfers between devices with their start and end apart: 10, of which 7 were waited for; matrix products, arithmetic and copies ran while one was open for 11% of the time, Pallas kernels for 0%

profile of v1, /device:TPU:0, one launch (start us, length us, event | category | flops | bytes accessed | tf_op | source)
XLA Modules:
  0.0 423.0 jit_solution(2728763809230795024)
XLA Ops:
  6.5 1.4 fusion.26
  11.5 2.2 constant_dynamic-slice_fusion.3
  13.7 0.3 copy.44
  14.0 1.4 copy.45
  15.4 1.2 pad_maximum_fusion
  16.7 0.0 all-gather.4.cloned.1.call-update
  16.7 0.0 all-gather.8.cloned.1.call-start
  16.8 1.0 constant_dynamic-slice_fusion.1
  17.7 0.1 copy.46
  17.9 0.1 copy.47
  18.0 0.7 pad_maximum_fusion.1
  18.7 0.0 all-gather.8.cloned.1.call-update
  18.8 0.0 copy-start.6
  18.8 0.0 copy-start.5
  18.8 0.0 all-gather.6.cloned.1.call-start
  18.8 150.9 %all-gather.4.cloned.1.call-done = bf16[5120,2,512]{0,2,1:T(8,128)(2,1)} async-done(((bf16[640,2,512]{0,2,1:T(8,128)(2,1)}), bf16[5120,2,512]{0,2,1:T(8,128)(2,1)}) %all-gather.4.cloned.1.call-update) | async-done | bytes 10485776 | tf_op jit(solution)/shard_map/all_gather | solution.py:24
  169.7 15.7 %fusion.1 = bf16[640,2,512]{0,2,1:T(8,128)(2,1)} fusion(bf16[5120,2,512]{0,2,1:T(8,128)(2,1)} %all-gather.4.cloned.1.call-done, bf16[2,640,5120]{2,1,0:T(8,128)(2,1)} %param.9), kind=kOutput, calls=%fused_computation.3 | convolution fusion | flops 6711541760 | bytes 24903680 | tf_op jit(solution)/shard_map/jsk,kjn->sjn/dot_general | solution.py:25
  185.4 0.0 all-gather.6.cloned.1.call-update
  185.6 0.6 dynamic-slice
  186.8 33.5 %all-gather.8.cloned.1.call-done = bf16[1024,2,512]{0,2,1:T(8,128)(2,1)} async-done(((bf16[128,2,512]{0,2,1:T(8,128)(2,1)}), bf16[1024,2,512]{0,2,1:T(8,128)(2,1)}) %all-gather.8.cloned.1.call-update) | async-done | bytes 2097168 | tf_op jit(solution)/shard_map/all_gather | solution.py:35
  220.3 2.3 fusion.2
  222.6 1.5 collective-permute-start.1
  224.1 3.3 collective-permute-start
  227.4 1.8 fusion.16
  229.2 11.9 %collective-permute-done.1 = bf16[128,2,512]{0,2,1:T(8,128)(2,1)S(1)} collective-permute-done((bf16[128,2,512]{0,2,1:T(8,128)(2,1)S(1)}, bf16[128,2,512]{0,2,1:T(8,128)(2,1)S(1)}, u32[]{:S(2)}, u32[]{:S(2)}) %collective-permute-start.1) | collective-permute-done | bytes 262176 | tf_op jit(solution)/shard_map/ppermute | solution.py:56
  241.1 2.5 collective-permute-start.3
  243.5 0.0 collective-permute-done
  243.5 2.2 collective-permute-start.2
  245.8 1.8 fusion.12
  247.6 1.8 fusion.14
  249.4 11.0 %collective-permute-done.3 = bf16[128,2,512]{0,2,1:T(8,128)(2,1)S(1)} collective-permute-done((bf16[128,2,512]{0,2,1:T(8,128)(2,1)S(1)}, bf16[128,2,512]{0,2,1:T(8,128)(2,1)S(1)}, u32[]{:S(2)}, u32[]{:S(2)}) %collective-permute-start.3) | collective-permute-done | bytes 262176 | tf_op jit(solution)/shard_map/ppermute | solution.py:56
  260.4 2.5 collective-permute-start.5
  262.8 0.7 collective-permute-done.2
  263.5 1.6 collective-permute-start.4
  265.1 1.8 fusion.10
  266.9 1.8 fusion.8
  268.6 7.4 %collective-permute-done.5 = bf16[128,2,512]{0,2,1:T(8,128)(2,1)S(1)} collective-permute-done((bf16[128,2,512]{0,2,1:T(8,128)(2,1)S(1)}, bf16[128,2,512]{0,2,1:T(8,128)(2,1)S(1)}, u32[]{:S(2)}, u32[]{:S(2)}) %collective-permute-start.5) | collective-permute-done | bytes 262176 | tf_op jit(solution)/shard_map/ppermute | solution.py:56
  276.1 0.0 collective-permute-start.6
  276.1 1.8 fusion.4
  277.8 0.0 collective-permute-done.4
  277.8 1.8 fusion.6
  279.6 108.0 %all-gather.6.cloned.1.call-done = bf16[5120,2,512]{0,2,1:T(8,128)(2,1)} async-done(((bf16[640,2,512]{0,2,1:T(8,128)(2,1)}), bf16[5120,2,512]{0,2,1:T(8,128)(2,1)}) %all-gather.6.cloned.1.call-update) | async-done | bytes 10485776 | tf_op jit(solution)/shard_map/all_gather | solution.py:32
  387.6 12.5 %fusion.27 = f32[2,512,512]{2,1,0:T(8,128)} fusion(bf16[5120,2,512]{0,2,1:T(8,128)(2,1)} %all-gather.6.cloned.1.call-done, bf16[2,512,5120]{2,1,0:T(8,128)(2,1)} %param.7), kind=kOutput, calls=%fused_computation.38 | convolution fusion | flops 5368709120 | bytes 23068672 | tf_op jit(solution)/shard_map/jti,ijn->jtn/dot_general | solution.py:29
  400.1 0.0 collective-permute-done.6
  400.2 5.2 %fusion = f32[512,512]{0,1:T(8,128)S(1)} fusion(f32[2,512,512]{2,1,0:T(8,128)} %fusion.27, f32[2,512,512]{1,2,0:T(8,128)} %fusion.4, f32[2,512,512]{1,2,0:T(8,128)} %fusion.6, f32[2,512,512]{1,2,0:T(8,128)} %fusion.8, f32[2,512,512]{1,2,0:T(8,128)S(1)} %copy-done.4, f32[2,512,512]{1,2,0:T(8,128)S(1)} %copy-done.2, f32[2,512,512]{1,2,0:T(8,128)S(1)} %copy-done.1, ...), kind=kOutput, calls=%fused_computation.1 | convolution fusion | flops 138674176 | bytes 18350084 | tf_op jit(solution)/shard_map/jti,ijn->jtn/dot_general | solution.py:67
  405.3 0.2 bitcast_reduce_fusion
  405.5 10.3 %all-reduce = f32[512,16]{0,1:T(8,128)S(1)} all-reduce(f32[512,16]{0,1:T(8,128)S(1)} %bitcast_reduce_fusion), channel_id=2, replica_groups=mesh['layer'=4,'shard'=8] {'layer'}, use_global_device_ids=true, to_apply=%region_2.3.clone | all-reduce | flops 8192 | bytes 65536
  415.9 0.6 constant_dynamic-slice_fusion.4
  (13 shorter events, 0.0 us)
Async XLA Ops:
  6.5 220.9 %copy-start = (bf16[2,512,1024]{2,1,0:T(8,128)(2,1)S(1)}, bf16[2,512,1024]{2,1,0:T(8,128)(2,1)}, u32[]{:S(2)}) copy-start(bf16[2,512,1024]{2,1,0:T(8,128)(2,1)} %param.8) | copy-start | bytes 6291460
  6.5 163.2 %all-gather.4.cloned.1.call-start = ((), (), s32[]{:S(2)}) async-start(), calls=%async_computation | async-start | bytes 11796480 | tf_op jit(solution)/shard_map/all_gather | solution.py:24
  16.7 203.6 %all-gather.8.cloned.1.call-start = ((), (), s32[]{:S(2)}) async-start(), calls=%async_computation.2 | async-start | bytes 2359296 | tf_op jit(solution)/shard_map/all_gather | solution.py:35
  18.8 166.8 %copy-start.6 = (u32[32]{0:T(128)S(1)}, u32[32]{0:T(128)}, u32[]{:S(2)}) copy-start(u32[32]{0:T(128)} %constant.87) | copy-start | bytes 388
  18.8 201.5 %copy-start.5 = (bf16[2,128,1024]{2,1,0:T(8,128)(2,1)S(1)}, bf16[2,128,1024]{2,1,0:T(8,128)(2,1)}, u32[]{:S(2)}) copy-start(bf16[2,128,1024]{2,1,0:T(8,128)(2,1)} %param.10) | copy-start | bytes 1572868
  18.8 368.9 %all-gather.6.cloned.1.call-start = ((), (), s32[]{:S(2)}) async-start(), calls=%async_computation.1 | async-start | bytes 11796480 | tf_op jit(solution)/shard_map/all_gather | solution.py:32
  222.6 18.4 %collective-permute-start.1 = (bf16[128,2,512]{0,2,1:T(8,128)(2,1)S(1)}, bf16[128,2,512]{0,2,1:T(8,128)(2,1)S(1)}, u32[]{:S(2)}, u32[]{:S(2)}) collective-permute-start(bf16[128,2,512]{0,2,1:T(8,128)(2,1)S(1)} %fusion.2), channel_id=1, source_target_pairs={{0,1},{1,2},{2,3},{3,4},{4,5},{5,6},{6,7},{7,0},{8,9},{9,10},{10,1... | collective-permute-start | bytes 786440 | tf_op jit(solution)/shard_map/ppermute | solution.py:56
  224.1 19.4 %collective-permute-start = (bf16[128,2,512]{0,2,1:T(8,128)(2,1)S(1)}, bf16[128,2,512]{0,2,1:T(8,128)(2,1)S(1)}, u32[]{:S(2)}, u32[]{:S(2)}) collective-permute-start(bf16[128,2,512]{0,2,1:T(8,128)(2,1)S(1)} %fusion.2), channel_id=1, source_target_pairs={{0,7},{1,0},{2,1},{3,2},{4,3},{5,4},{6,5},{7,6},{8,15},{9,8},{10,9... | collective-permute-start | bytes 786440 | tf_op jit(solution)/shard_map/ppermute | solution.py:58
  241.1 19.3 %collective-permute-start.3 = (bf16[128,2,512]{0,2,1:T(8,128)(2,1)S(1)}, bf16[128,2,512]{0,2,1:T(8,128)(2,1)S(1)}, u32[]{:S(2)}, u32[]{:S(2)}) collective-permute-start(bf16[128,2,512]{0,2,1:T(8,128)(2,1)S(1)} %collective-permute-done.1), channel_id=1, source_target_pairs={{0,1},{1,2},{2,3},{3,4},{4,5},{5,6},{6,7},{7,0},{8,9},{9,10},{10,1... | collective-permute-start | bytes 786440 | tf_op jit(solution)/shard_map/ppermute | solution.py:56
  243.5 19.9 %collective-permute-start.2 = (bf16[128,2,512]{0,2,1:T(8,128)(2,1)S(1)}, bf16[128,2,512]{0,2,1:T(8,128)(2,1)S(1)}, u32[]{:S(2)}, u32[]{:S(2)}) collective-permute-start(bf16[128,2,512]{0,2,1:T(8,128)(2,1)S(1)} %collective-permute-done), channel_id=1, source_target_pairs={{0,7},{1,0},{2,1},{3,2},{4,3},{5,4},{6,5},{7,6},{8,15},{9,8},{10,9... | collective-permute-start | bytes 786440 | tf_op jit(solution)/shard_map/ppermute | solution.py:58
  260.4 15.7 %collective-permute-start.5 = (bf16[128,2,512]{0,2,1:T(8,128)(2,1)S(1)}, bf16[128,2,512]{0,2,1:T(8,128)(2,1)S(1)}, u32[]{:S(2)}, u32[]{:S(2)}) collective-permute-start(bf16[128,2,512]{0,2,1:T(8,128)(2,1)S(1)} %collective-permute-done.3), channel_id=1, source_target_pairs={{0,1},{1,2},{2,3},{3,4},{4,5},{5,6},{6,7},{7,0},{8,9},{9,10},{10,1... | collective-permute-start | bytes 786440 | tf_op jit(solution)/shard_map/ppermute | solution.py:56
  263.5 14.4 %collective-permute-start.4 = (bf16[128,2,512]{0,2,1:T(8,128)(2,1)S(1)}, bf16[128,2,512]{0,2,1:T(8,128)(2,1)S(1)}, u32[]{:S(2)}, u32[]{:S(2)}) collective-permute-start(bf16[128,2,512]{0,2,1:T(8,128)(2,1)S(1)} %collective-permute-done.2), channel_id=1, source_target_pairs={{0,7},{1,0},{2,1},{3,2},{4,3},{5,4},{6,5},{7,6},{8,15},{9,8},{10,9... | collective-permute-start | bytes 786440 | tf_op jit(solution)/shard_map/ppermute | solution.py:58
  276.1 124.1 %collective-permute-start.6 = (bf16[128,2,512]{0,2,1:T(8,128)(2,1)S(1)}, bf16[128,2,512]{0,2,1:T(8,128)(2,1)S(1)}, u32[]{:S(2)}, u32[]{:S(2)}) collective-permute-start(bf16[128,2,512]{0,2,1:T(8,128)(2,1)S(1)} %collective-permute-done.5), channel_id=1, source_target_pairs={{0,1},{1,2},{2,3},{3,4},{4,5},{5,6},{6,7},{7,0},{8,9},{9,10},{10,1... | collective-permute-start | bytes 786440 | tf_op jit(solution)/shard_map/ppermute | solution.py:56
  387.6 12.5 %copy-start.1 = (f32[2,512,512]{1,2,0:T(8,128)S(1)}, f32[2,512,512]{1,2,0:T(8,128)}, u32[]{:S(2)}) copy-start(f32[2,512,512]{1,2,0:T(8,128)} %fusion.16) | copy-start | bytes 6291460
  387.6 12.5 %copy-start.2 = (f32[2,512,512]{1,2,0:T(8,128)S(1)}, f32[2,512,512]{1,2,0:T(8,128)}, u32[]{:S(2)}) copy-start(f32[2,512,512]{1,2,0:T(8,128)} %fusion.12) | copy-start | bytes 6291460
  387.6 12.5 %copy-start.3 = (f32[2,512,512]{1,2,0:T(8,128)S(1)}, f32[2,512,512]{1,2,0:T(8,128)}, u32[]{:S(2)}) copy-start(f32[2,512,512]{1,2,0:T(8,128)} %fusion.14) | copy-start | bytes 6291460
  387.6 12.5 %copy-start.4 = (f32[2,512,512]{1,2,0:T(8,128)S(1)}, f32[2,512,512]{1,2,0:T(8,128)}, u32[]{:S(2)}) copy-start(f32[2,512,512]{1,2,0:T(8,128)} %fusion.10) | copy-start | bytes 6291460
Sparse Core Ops, SparseCore 0:
  16.8 152.8 all-gather.3
  171.7 48.5 all-gather.7
  222.5 165.0 all-gather.5
